TPU v7x, 256 devices: a whole 4x4x8 slice. The times are simulated.
256 devices in a mesh: ctx: 64 (over z, x, core), kvh: 4 (over y).
Axes of the slice: x: 4, y: 4, z: 8, core: 2. Of those that a mesh axis runs over, the one named last changes fastest.
Arguments:
- query_rows: bfloat16 [16384, 4096], P('ctx', 'kvh'), may hold values from -6 to 6
- key_rows: bfloat16 [16384, 1024], P('ctx', 'kvh'), may hold values from -6 to 6
- value_rows: bfloat16 [16384, 1024], P('ctx', 'kvh'), may hold values from -60 to 60
- grad_out: bfloat16 [16384, 4096], P('ctx', 'kvh'), may hold values from -6 to 6
- chosen: int32 [32, 2], replicated, may hold values from 0 to 31, as said below
Outputs:
- normed: bfloat16 [16384, 4096], P('ctx', 'kvh')
- grad_query: bfloat16 [16384, 4096], P('ctx', 'kvh')
- grad_key: bfloat16 [16384, 1024], P('ctx', 'kvh')
- grad_value: bfloat16 [16384, 1024], P('ctx', 'kvh')
Inputs may be any that keep to these rules, and one draw needn't show every extreme that they name: For query block b with b >= 2, chosen[b, 0] and chosen[b, 1] are distinct and below b. chosen[1, 0] = 0. Slots of blocks 0 and 1 that have no earlier block hold 31.
All inputs are finite; a program needn't handle non-finite values.
Results may differ from a plain program's by a relative error of at most 0.013.
Values may be sent and summed in bfloat16 or wider, within the bound.
A program may use at most 128 MiB of HBM per device.

v0:
```python
import functools
import math

import jax
import jax.numpy as jnp
from jax import lax
from jax.experimental import pallas as pl
from jax.experimental.pallas import tpu as pltpu
from jax.sharding import PartitionSpec as P

HEADS = 32
HEAD_DIM = 128
EPSILON = 1e-06
SCALE = 1.0 / math.sqrt(HEAD_DIM)
SCALE2 = SCALE * math.log2(math.e)
MESH = pl.DeviceIdType.MESH
F32 = jnp.float32
BF16 = jnp.bfloat16
NEG = -jnp.inf


def dot(left, right):
    return jnp.dot(left, right, preferred_element_type=F32)


def aligned(start, size, step):
    return pl.ds(pl.multiple_of(start, step), size)


def kernel(
    blocks, rows, group, kvh,
    chosen, q_in, k_in, v_in, g_in,
    normed_out, gq_out, gk_out, gv_out,
    qs, gos, kv, vtx, kt, qt, gt, held, picked, probs, maxes, parts, weights, att_wide,
    stat_send, stat_recv, gat, ga, delta, dqt, dkv, dkv_send, arrived, table, totals, home,
    nrm, gq, gkv,
    local_sem, swap_send, swap_recv, hop_send, hop_recv, stat_sems, out_local, out_send, out_recv,
):
    hd = HEAD_DIM
    block = 2 * rows
    piece = block // blocks
    width = group * hd
    ctx = lax.axis_index("ctx")
    y = lax.axis_index("kvh")
    mine = ctx // 2
    core = lax.rem(ctx, 2)
    other = 1 - core
    partner = (2 * mine + other, y)
    members = 2 * kvh
    slot = 2 * y + core

    def peer(step):
        return lax.rem(mine + step, blocks)

    def member(step):
        at = lax.rem(slot + step, members)
        return (2 * mine + lax.rem(at, 2), at // 2)

    def drain(ref, sem):
        pltpu.make_async_copy(ref, ref, sem).wait()

    def send(src, dst, send_sem, recv_sem, device):
        pltpu.make_async_remote_copy(
            src_ref=src, dst_ref=dst, send_sem=send_sem, recv_sem=recv_sem,
            device_id=device, device_id_type=MESH,
        ).start()

    own_rows = aligned(core * rows, rows, rows)
    other_rows = aligned(other * rows, rows, rows)
    own_head = aligned(core * hd, hd, hd)
    other_head = aligned(other * hd, hd, hd)
    own_group = aligned(core * width, width, width)
    other_group = aligned(other * width, width, width)
    k_lanes = pl.ds(0, hd)
    v_lanes = pl.ds(hd, hd)

    fetches = [
        pltpu.make_async_copy(k_in.at[:, own_head], kv.at[own_rows, k_lanes], local_sem.at[0]),
        pltpu.make_async_copy(v_in.at[:, own_head], kv.at[own_rows, v_lanes], local_sem.at[1]),
        pltpu.make_async_copy(q_in.at[:, own_group], qs.at[own_rows, :], local_sem.at[2]),
        pltpu.make_async_copy(g_in.at[:, own_group], gos.at[own_rows, :], local_sem.at[3]),
    ]
    for fetch in fetches:
        fetch.start()

    barrier = pltpu.get_barrier_semaphore()

    @pl.loop(1, blocks)
    def _(step):
        pl.semaphore_signal(
            barrier, inc=1, device_id=(2 * peer(step) + core, y), device_id_type=MESH
        )

    @pl.loop(1, members)
    def _(step):
        pl.semaphore_signal(barrier, inc=1, device_id=member(step), device_id_type=MESH)

    pl.semaphore_wait(barrier, blocks + members - 2)

    swaps = [
        (k_in.at[:, other_head], kv.at[own_rows, k_lanes]),
        (v_in.at[:, other_head], kv.at[own_rows, v_lanes]),
        (q_in.at[:, other_group], qs.at[own_rows, :]),
        (g_in.at[:, other_group], gos.at[own_rows, :]),
    ]
    for number, (src, dst) in enumerate(swaps):
        send(src, dst, swap_send.at[number], swap_recv.at[number], partner)
    fetches[0].wait()
    fetches[1].wait()

    def scatter_half(half):
        count = blocks // 2

        @pl.loop(0, count)
        def _(step):
            to = half * count + lax.rem(step + mine, count)

            @pl.when(to != mine)
            def _():
                send(
                    kv.at[aligned(piece * to, piece, piece), :], held.at[mine],
                    hop_send.at[0], hop_recv.at[0], (2 * to + core, y),
                )

    scatter_half(core)
    drain(kv.at[other_rows, k_lanes], swap_recv.at[0])
    drain(kv.at[other_rows, v_lanes], swap_recv.at[1])
    scatter_half(other)
    held[mine] = kv[aligned(piece * mine, piece, piece), :]

    fetches[2].wait()
    fetches[3].wait()
    drain(qs.at[other_rows, :], swap_recv.at[2])
    drain(gos.at[other_rows, :], swap_recv.at[3])

    def turn_keys(section):
        at = pl.ds(section * block, block)
        kt[section] = kv[at, 0:hd].T
        vtx[section, 0:hd, :] = kv[at, hd : 2 * hd].T
        vtx[section, hd : hd + 16, :] = jnp.ones((16, block), BF16)

    def forward(section, head):
        keys = kv[section * block : (section + 1) * block, 0:hd]
        scores = dot(keys, qt[head])
        if section == 0:
            key_at = lax.broadcasted_iota(jnp.int32, (block, block), 0)
            row_at = lax.broadcasted_iota(jnp.int32, (block, block), 1)
            key_order = 2 * lax.rem(key_at, rows) + key_at // rows
            row_order = 2 * lax.rem(row_at, rows) + row_at // rows
            scores = jnp.where(key_order <= row_order, scores, NEG)
        top = jnp.max(scores, axis=0, keepdims=True)
        terms = jnp.exp2((scores - top) * SCALE2).astype(BF16)
        probs[section, head] = terms
        maxes[section, head] = jnp.broadcast_to(top, (8, block))
        parts[section, head] = dot(vtx[section], terms)

    turn_keys(0)

    @pl.loop(0, group)
    def _(head):
        lanes = aligned(head * hd, hd, hd)
        qt[head] = qs[:, lanes].T
        gt[head] = gos[:, lanes].T

    for pick in range(2):
        lane_owner = lax.broadcasted_iota(jnp.int32, (8, block), 1) // piece

        def fill(reader, owners):
            choice = chosen[reader, pick]
            choice = jnp.where(choice < reader, choice, -1)
            return jnp.where(lane_owner == reader, choice, owners)

        owners = lax.fori_loop(0, blocks, fill, jnp.full((8, block), -1, jnp.int32))
        row_at = lax.broadcasted_iota(jnp.int32, (block, block), 0)
        lane_at = lax.broadcasted_iota(jnp.int32, (block, block), 1)
        wanted = owners[0:1] * piece + lax.rem(lane_at, piece)
        table[pick] = (row_at == wanted).astype(F32).astype(BF16)

    forward(0, 0)

    drain(held.at[pl.ds(0, blocks - 1)], hop_recv.at[0])
    for pick in range(2):
        base = (1 + pick) * block

        @pl.loop(1, blocks)
        def _(step):
            to = peer(step)
            picked[pick, to] = held[chosen[to, pick]]
            send(
                picked.at[pick, to], kv.at[aligned(base + piece * mine, piece, piece), :],
                hop_send.at[1 + pick], hop_recv.at[1 + pick], (2 * to + core, y),
            )

        kv[aligned(base + piece * mine, piece, piece), :] = held[chosen[mine, pick]]

    @pl.loop(1, group)
    def _(head):
        forward(0, head)

    for pick in range(2):
        base = (1 + pick) * block
        drain(kv.at[pl.ds(base, block - piece), :], hop_recv.at[1 + pick])
        turn_keys(1 + pick)

        @pl.loop(0, group)
        def _(head):
            forward(1 + pick, head)

    valid = [chosen[mine, pick] < mine for pick in range(2)]

    def merge(head, sums):
        top_own = maxes[0, head, 0:1]
        tops = [top_own] + [
            jnp.where(valid[pick], maxes[1 + pick, head, 0:1], NEG) for pick in range(2)
        ]
        top = jnp.maximum(jnp.maximum(tops[0], tops[1]), tops[2])
        ratios = [jnp.exp2((value - top) * SCALE2) for value in tops]
        total = sum(
            ratio * parts[section, head, hd : hd + 1] for section, ratio in enumerate(ratios)
        )
        inverse = 1.0 / total
        shares = [ratio * inverse for ratio in ratios]
        for section in range(3):
            weights[section, head] = jnp.broadcast_to(shares[section], (8, block))
        wide = sum(share * parts[section, head, 0:hd] for section, share in enumerate(shares))
        att_wide[head] = wide
        rounded = wide.astype(BF16).astype(F32)
        upstream = gt[head].astype(F32)
        return (
            sums[0] + jnp.sum(rounded * rounded, axis=0, keepdims=True),
            sums[1] + jnp.sum(rounded * upstream, axis=0, keepdims=True),
        )

    zero_row = jnp.zeros((1, block), F32)
    square_sum, cross_sum = lax.fori_loop(0, group, merge, (zero_row, zero_row))
    stat_send[...] = jnp.concatenate(
        [square_sum, cross_sum, jnp.zeros((6, block), F32)], axis=0
    )

    @pl.loop(1, members)
    def _(step):
        send(stat_send, stat_recv.at[slot], stat_sems.at[0], stat_sems.at[1], member(step))

    stat_recv[slot] = stat_send[...]
    drain(stat_recv.at[pl.ds(0, members - 1)], stat_sems.at[1])
    stats = stat_recv[0]
    for at in range(1, members):
        stats = stats + stat_recv[at]
    features = HEADS * HEAD_DIM
    rscale = lax.rsqrt(stats[0:1] / features + EPSILON)
    factor = rscale * rscale * rscale * (stats[1:2] / features)

    @pl.loop(0, group)
    def _(head):
        wide = att_wide[head]
        rounded = wide.astype(BF16).astype(F32)
        upstream = gt[head].astype(F32)
        lanes = aligned(head * hd, hd, hd)
        grad = (rscale * upstream - rounded * factor).astype(BF16)
        gat[head] = grad
        ga[head] = grad.T
        delta[head] = jnp.broadcast_to(
            jnp.sum(wide * grad.astype(F32), axis=0, keepdims=True), (8, block)
        )
        nrm[:, lanes] = (rounded * rscale).astype(BF16).T

    def hand_out(number, buffer, out):
        send(
            buffer.at[other_rows, :], out.at[:, own_group],
            out_send.at[number], out_recv.at[number], partner,
        )
        keep = pltpu.make_async_copy(
            buffer.at[own_rows, :], out.at[:, own_group], out_local.at[number]
        )
        keep.start()
        return keep

    keeps = [hand_out(0, nrm, normed_out)]
    dqt[...] = jnp.zeros_like(dqt)

    def backward(section, head):
        values = kv[section * block : (section + 1) * block, hd : 2 * hd]
        dprob = dot(values, gat[head])
        share = probs[section, head].astype(F32) * weights[section, head, 0:1]
        dscore = (share * (dprob - delta[head, 0:1])).astype(BF16)
        lanes = aligned(head * hd, hd, hd)
        dqt[head] += dot(kt[section], dscore)
        dkv[section, :, 0:hd] += dot(dscore, qs[:, lanes])
        dkv[section, :, hd : 2 * hd] += dot(share.astype(BF16), ga[head])

    def backward_section(section):
        dkv[section] = jnp.zeros((block, 2 * hd), F32)

        @pl.loop(0, group)
        def _(head):
            backward(section, head)

    for pick in range(2):
        section = 1 + pick
        backward_section(section)
        dkv_send[pick, :, 0:hd] = (dkv[section, :, 0:hd] * SCALE).astype(BF16)
        dkv_send[pick, :, hd : 2 * hd] = dkv[section, :, hd : 2 * hd].astype(BF16)

        @pl.loop(1, blocks)
        def _(step):
            to = peer(step)
            send(
                dkv_send.at[pick, aligned(piece * to, piece, piece), :],
                arrived.at[pick, aligned(piece * mine, piece, piece), :],
                hop_send.at[3 + pick], hop_recv.at[3 + pick], (2 * to + core, y),
            )

        arrived[pick, aligned(piece * mine, piece, piece), :] = dkv_send[
            pick, aligned(piece * mine, piece, piece), :
        ]

    backward_section(0)

    @pl.loop(0, group)
    def _(head):
        lanes = aligned(head * hd, hd, hd)
        gq[:, lanes] = (dqt[head] * SCALE).astype(BF16).T

    keeps.append(hand_out(1, gq, gq_out))

    for pick in range(2):
        drain(arrived.at[pick, pl.ds(0, block - piece), :], hop_recv.at[3 + pick])
    totals[...] = (dot(table[0], arrived[0]) + dot(table[1], arrived[1])).astype(BF16)

    @pl.loop(1, blocks)
    def _(step):
        to = peer(step)
        send(
            totals.at[aligned(piece * to, piece, piece), :],
            home.at[aligned(piece * mine, piece, piece), :],
            hop_send.at[5], hop_recv.at[5], (2 * to + core, y),
        )

    home[aligned(piece * mine, piece, piece), :] = totals[aligned(piece * mine, piece, piece), :]
    drain(home.at[pl.ds(0, block - piece), :], hop_recv.at[5])
    gkv[:, 0:hd] = (dkv[0, :, 0:hd] * SCALE + home[:, 0:hd].astype(F32)).astype(BF16)
    gkv[:, hd : 2 * hd] = (
        dkv[0, :, hd : 2 * hd] + home[:, hd : 2 * hd].astype(F32)
    ).astype(BF16)

    for number, (lanes, out) in enumerate(((k_lanes, gk_out), (v_lanes, gv_out))):
        send(
            gkv.at[other_rows, lanes], out.at[:, own_head],
            out_send.at[2 + number], out_recv.at[2 + number], partner,
        )
        keep = pltpu.make_async_copy(
            gkv.at[own_rows, lanes], out.at[:, own_head], out_local.at[2 + number]
        )
        keep.start()
        keeps.append(keep)

    for keep in keeps:
        keep.wait()
    for number, (src, dst) in enumerate(swaps):
        drain(src, swap_send.at[number])
    drain(held.at[pl.ds(0, blocks - 1)], hop_send.at[0])
    for pick in range(2):
        drain(picked.at[pick, pl.ds(0, blocks - 1)], hop_send.at[1 + pick])
        drain(dkv_send.at[pick, pl.ds(0, block - piece), :], hop_send.at[3 + pick])
    drain(totals.at[pl.ds(0, block - piece), :], hop_send.at[5])
    drain(stat_recv.at[pl.ds(0, members - 1)], stat_sems.at[0])
    for number, (buffer, out) in enumerate(((nrm, normed_out), (gq, gq_out))):
        drain(buffer.at[other_rows, :], out_send.at[number])
        drain(out.at[:, other_group], out_recv.at[number])
    for number, (lanes, out) in enumerate(((k_lanes, gk_out), (v_lanes, gv_out))):
        drain(gkv.at[other_rows, lanes], out_send.at[2 + number])
        drain(out.at[:, other_head], out_recv.at[2 + number])


def shards(query_rows, key_rows, value_rows, grad_out, chosen):
    blocks = chosen.shape[0]
    rows, kv_width = key_rows.shape
    group = query_rows.shape[1] // kv_width
    kvh = lax.axis_size("kvh")
    hd = HEAD_DIM
    block = 2 * rows
    piece = block // blocks
    width = group * hd
    anywhere = pl.BlockSpec(memory_space=pl.ANY)
    scratch = [
        pltpu.VMEM((block, width), BF16),
        pltpu.VMEM((block, width), BF16),
        pltpu.VMEM((3 * block, 2 * hd), BF16),
        pltpu.VMEM((3, hd + 16, block), BF16),
        pltpu.VMEM((3, hd, block), BF16),
        pltpu.VMEM((group, hd, block), BF16),
        pltpu.VMEM((group, hd, block), BF16),
        pltpu.VMEM((blocks, piece, 2 * hd), BF16),
        pltpu.VMEM((2, blocks, piece, 2 * hd), BF16),
        pltpu.VMEM((3, group, block, block), BF16),
        pltpu.VMEM((3, group, 8, block), F32),
        pltpu.VMEM((3, group, hd + 16, block), F32),
        pltpu.VMEM((3, group, 8, block), F32),
        pltpu.VMEM((group, hd, block), F32),
        pltpu.VMEM((8, block), F32),
        pltpu.VMEM((2 * kvh, 8, block), F32),
        pltpu.VMEM((group, hd, block), BF16),
        pltpu.VMEM((group, block, hd), BF16),
        pltpu.VMEM((group, 8, block), F32),
        pltpu.VMEM((group, hd, block), F32),
        pltpu.VMEM((3, block, 2 * hd), F32),
        pltpu.VMEM((2, block, 2 * hd), BF16),
        pltpu.VMEM((2, block, 2 * hd), BF16),
        pltpu.VMEM((2, block, block), BF16),
        pltpu.VMEM((block, 2 * hd), BF16),
        pltpu.VMEM((block, 2 * hd), BF16),
        pltpu.VMEM((block, width), BF16),
        pltpu.VMEM((block, width), BF16),
        pltpu.VMEM((block, 2 * hd), BF16),
        pltpu.SemaphoreType.DMA((4,)),
        pltpu.SemaphoreType.DMA((4,)),
        pltpu.SemaphoreType.DMA((4,)),
        pltpu.SemaphoreType.DMA((6,)),
        pltpu.SemaphoreType.DMA((6,)),
        pltpu.SemaphoreType.DMA((2,)),
        pltpu.SemaphoreType.DMA((4,)),
        pltpu.SemaphoreType.DMA((4,)),
        pltpu.SemaphoreType.DMA((4,)),
    ]
    return pl.pallas_call(
        functools.partial(kernel, blocks, rows, group, kvh),
        out_shape=(
            jax.ShapeDtypeStruct(query_rows.shape, BF16),
            jax.ShapeDtypeStruct(query_rows.shape, BF16),
            jax.ShapeDtypeStruct(key_rows.shape, BF16),
            jax.ShapeDtypeStruct(key_rows.shape, BF16),
        ),
        in_specs=[pl.BlockSpec(memory_space=pltpu.SMEM)] + [anywhere] * 4,
        out_specs=(anywhere,) * 4,
        scratch_shapes=scratch,
        compiler_params=pltpu.CompilerParams(
            collective_id=0, has_side_effects=True, vmem_limit_bytes=60 * 2**20
        ),
        name="moba",
    )(chosen, query_rows, key_rows, value_rows, grad_out)


def solution(mesh):
    return jax.shard_map(
        shards,
        mesh=mesh,
        in_specs=(P("ctx", "kvh"), P("ctx", "kvh"), P("ctx", "kvh"), P("ctx", "kvh"), P()),
        out_specs=(P("ctx", "kvh"), P("ctx", "kvh"), P("ctx", "kvh"), P("ctx", "kvh")),
        check_vma=False,
    )
```

profile of v0, /device:TPU:1, one launch (start us, length us, event | category | flops | bytes accessed | tf_op | source)
XLA Modules:
  0.0 80.9 jit_solution(5012813450333714610)
XLA Ops:
  0.6 1.4 %copy.9.chosen = s32[32,2]{1,0:T(8,128)} copy(s32[32,2]{0,1:T(2,128)} %param.9) | data formatting | bytes 512 | tf_op args[4]
  2.0 74.3 %moba.1 = (bf16[256,1024]{1,0:T(8,128)(2,1)}, bf16[256,1024]{1,0:T(8,128)(2,1)}, bf16[256,256]{1,0:T(8,128)(2,1)}, bf16[256,256]{1,0:T(8,128)(2,1)}) custom-call(s32[32,2]{1,0:T(8,128)} %copy.9.chosen, bf16[256,1024]{1,0:T(8,128)(2,1)} %q_in.1, bf16[256,256]{1,0:T(8,128)(2,1)} %k_in.1, bf16[256,256]{1,0:T(8,128)(2,1)} %v_in.1, bf16[256,1024]{1,0:T(8,128)(2,1)} %g_in.1), custom_call_target="tpu_custom_call" | custom-call | tf_op jit(solution)/shard_map/moba/pallas_call | solution.py:425
  76.3 0.0 copy-start
  76.3 1.9 %copy.14 = bf16[256,1024]{1,0:T(8,128)(2,1)} copy(bf16[256,1024]{1,0:T(8,128)(2,1)} %get-tuple-element.8) | data formatting | bytes 1048576
  78.2 0.0 copy-done
  78.2 0.0 copy-start.2
  78.2 0.8 copy.15
  79.0 0.2 copy-done.2
  79.2 0.0 copy-start.1
  79.2 0.7 copy.16
  79.9 0.3 copy-done.1
  80.2 0.7 copy.17
Async XLA Ops:
  76.3 1.9 %copy-start = (bf16[256,1024]{1,0:T(8,128)(2,1)S(1)}, bf16[256,1024]{1,0:T(8,128)(2,1)}, u32[]{:S(2)}) copy-start(bf16[256,1024]{1,0:T(8,128)(2,1)} %get-tuple-element.9) | copy-start | bytes 1572868
  78.2 1.0 %copy-start.2 = (bf16[256,256]{1,0:T(8,128)(2,1)S(1)}, bf16[256,256]{1,0:T(8,128)(2,1)}, u32[]{:S(2)}) copy-start(bf16[256,256]{1,0:T(8,128)(2,1)} %get-tuple-element.10) | copy-start | bytes 393220
  79.2 1.0 %copy-start.1 = (bf16[256,256]{1,0:T(8,128)(2,1)S(1)}, bf16[256,256]{1,0:T(8,128)(2,1)}, u32[]{:S(2)}) copy-start(bf16[256,256]{1,0:T(8,128)(2,1)} %get-tuple-element.11) | copy-start | bytes 393220
where the time goes:
time: 81.1 us; the launch traced here: 80.9 us
  Pallas kernels  74.3 us (92%)
  local copies, waits for them, and re-layouts  5.92 us (7%)
    pallas_call x1, Pallas kernels, shards(): pl.pallas_call(functools.partial(kernel, blocks, rows, group, kvh), out_s...  74.3 us
    unnamed x11, local copies, waits for them, and re-layouts  5.92 us

commit v1 on v0

v1 whole, which is shorter than its diff:
```python
import functools
import math

import jax
import jax.numpy as jnp
from jax import lax
from jax.experimental import pallas as pl
from jax.experimental.pallas import tpu as pltpu
from jax.sharding import PartitionSpec as P

HEADS = 32
HEAD_DIM = 128
EPSILON = 1e-06
SCALE = 1.0 / math.sqrt(HEAD_DIM)
SCALE2 = SCALE * math.log2(math.e)
MESH = pl.DeviceIdType.MESH
F32 = jnp.float32
BF16 = jnp.bfloat16
NEG = -jnp.inf


def dot(left, right):
    return jnp.dot(left, right, preferred_element_type=F32)


def aligned(start, size, step):
    return pl.ds(pl.multiple_of(start, step), size)


def kernel(
    blocks, rows, group, kvh,
    chosen, q_in, k_in, v_in, g_in,
    normed_out, gq_out, part_k, part_v, home_k, home_v,
    qs, gos, ks, vs, vtx, kt, qt, gt, held_k, held_v, picked_k, picked_v, probs, maxes, parts,
    weights, att_wide, stat_send, stat_recv, gat, ga, delta, dqt, dk, dv, dk_send, dv_send,
    arrived_k, arrived_v, table, totals_k, totals_v, nrm, gq,
    local_sem, swap_send, swap_recv, hop_send, hop_recv, stat_sems, out_local, out_send, out_recv,
):
    hd = HEAD_DIM
    block = 2 * rows
    piece = block // blocks
    width = group * hd
    ctx = lax.axis_index("ctx")
    y = lax.axis_index("kvh")
    mine = ctx // 2
    core = lax.rem(ctx, 2)
    other = 1 - core
    partner = (2 * mine + other, y)
    far = 2 * (kvh - 1)
    half_blocks = blocks // 2
    upper = mine // half_blocks

    def peer(step):
        return lax.rem(mine + step, blocks)

    def far_member(step):
        return (2 * mine + lax.rem(step, 2), lax.rem(y + 1 + step // 2, kvh))

    def drain(ref, sem):
        pltpu.make_async_copy(ref, ref, sem).wait()

    def send(src, dst, send_sem, recv_sem, device):
        pltpu.make_async_remote_copy(
            src_ref=src, dst_ref=dst, send_sem=send_sem, recv_sem=recv_sem,
            device_id=device, device_id_type=MESH,
        ).start()

    def signal(device):
        pl.semaphore_signal(barrier, inc=1, device_id=device, device_id_type=MESH)

    own_rows = aligned(core * rows, rows, rows)
    other_rows = aligned(other * rows, rows, rows)
    own_head = aligned(core * hd, hd, hd)
    other_head = aligned(other * hd, hd, hd)
    own_group = aligned(core * width, width, width)
    other_group = aligned(other * width, width, width)
    my_piece = aligned(piece * mine, piece, piece)

    fetches = [
        pltpu.make_async_copy(k_in.at[:, own_head], ks.at[0, own_rows, :], local_sem.at[0]),
        pltpu.make_async_copy(v_in.at[:, own_head], vs.at[0, own_rows, :], local_sem.at[1]),
        pltpu.make_async_copy(q_in.at[:, own_group], qs.at[own_rows, :], local_sem.at[2]),
        pltpu.make_async_copy(g_in.at[:, own_group], gos.at[own_rows, :], local_sem.at[3]),
    ]
    for fetch in fetches:
        fetch.start()

    barrier = pltpu.get_barrier_semaphore()

    @pl.loop(1, 2 * blocks)
    def _(step):
        signal((lax.rem(ctx + step, 2 * blocks), y))

    @pl.loop(0, far)
    def _(step):
        signal(far_member(step))

    pl.semaphore_wait(barrier, 2 * blocks - 1 + far)

    swaps = [
        (k_in.at[:, other_head], ks.at[0, own_rows, :]),
        (v_in.at[:, other_head], vs.at[0, own_rows, :]),
        (q_in.at[:, other_group], qs.at[own_rows, :]),
        (g_in.at[:, other_group], gos.at[own_rows, :]),
    ]
    for number, (src, dst) in enumerate(swaps):
        send(src, dst, swap_send.at[number], swap_recv.at[number], partner)

    def scatter(number, source, held):
        def scatter_half(half):
            @pl.loop(0, half_blocks)
            def _(step):
                to = half * half_blocks + lax.rem(step + mine, half_blocks)

                @pl.when(to != mine)
                def _():
                    send(
                        source.at[0, aligned(piece * to, piece, piece), :], held.at[mine],
                        hop_send.at[number], hop_recv.at[number], (2 * to + core, y),
                    )

        fetches[number].wait()
        scatter_half(core)
        drain(source.at[0, other_rows, :], swap_recv.at[number])
        scatter_half(other)
        held[mine] = source[0, my_piece, :]

    scatter(0, ks, held_k)
    scatter(1, vs, held_v)

    for number, target in ((2, qs), (3, gos)):
        fetches[number].wait()
        drain(target.at[other_rows, :], swap_recv.at[number])

    def turn_keys(section):
        kt[section] = ks[section].T

    def turn_values(section):
        vtx[section, 0:hd, :] = vs[section].T
        vtx[section, hd : hd + 16, :] = jnp.ones((16, block), BF16)

    def score(section, head):
        scores = dot(ks[section], qt[head])
        if section == 0:
            key_at = lax.broadcasted_iota(jnp.int32, (block, block), 0)
            row_at = lax.broadcasted_iota(jnp.int32, (block, block), 1)
            key_order = 2 * lax.rem(key_at, rows) + key_at // rows
            row_order = 2 * lax.rem(row_at, rows) + row_at // rows
            scores = jnp.where(key_order <= row_order, scores, NEG)
        top = jnp.max(scores, axis=0, keepdims=True)
        terms = jnp.exp2((scores - top) * SCALE2).astype(BF16)
        probs[section, head] = terms
        maxes[section, head] = jnp.broadcast_to(top, (8, block))
        return terms

    def deliver(number, held, picked, target):
        drain(held.at[pl.ds(0, blocks - 1)], hop_recv.at[number])

        @pl.loop(1, blocks)
        def _(step):
            to = peer(step)
            for pick in range(2):
                picked[to, pick] = held[chosen[pick, to]]
            send(
                picked.at[to], target.at[pl.ds(1, 2), my_piece, :],
                hop_send.at[2 + number], hop_recv.at[2 + number], (2 * to + core, y),
            )

        for pick in range(2):
            target[1 + pick, my_piece, :] = held[chosen[pick, mine]]

    turn_keys(0)

    @pl.loop(0, group)
    def _(head):
        qt[head] = qs[:, aligned(head * hd, hd, hd)].T

    deliver(0, held_k, picked_k, ks)
    turn_values(0)

    @pl.loop(0, group)
    def _(head):
        gt[head] = gos[:, aligned(head * hd, hd, hd)].T

    deliver(1, held_v, picked_v, vs)

    @pl.loop(0, group)
    def _(head):
        parts[0, head] = dot(vtx[0], score(0, head))

    for pick in range(2):
        lane_owner = lax.broadcasted_iota(jnp.int32, (8, block), 1) // piece

        def fill(reader, owners):
            choice = chosen[pick, reader]
            choice = jnp.where(choice < reader, choice, -1)
            return jnp.where(lane_owner == reader, choice, owners)

        owners = lax.fori_loop(0, blocks, fill, jnp.full((8, block), -1, jnp.int32))
        row_at = lax.broadcasted_iota(jnp.int32, (block, block), 0)
        lane_at = lax.broadcasted_iota(jnp.int32, (block, block), 1)
        wanted = owners[0:1] * piece + lax.rem(lane_at, piece)
        table[pick] = (row_at == wanted).astype(F32).astype(BF16)

    drain(ks.at[pl.ds(1, 2), pl.ds(0, block - piece), :], hop_recv.at[2])
    for pick in range(2):
        @pl.loop(0, group)
        def _(head):
            score(1 + pick, head)

        turn_keys(1 + pick)

    drain(vs.at[pl.ds(1, 2), pl.ds(0, block - piece), :], hop_recv.at[3])
    for pick in range(2):
        turn_values(1 + pick)

        @pl.loop(0, group)
        def _(head):
            parts[1 + pick, head] = dot(vtx[1 + pick], probs[1 + pick, head])

    valid = [chosen[pick, mine] < mine for pick in range(2)]

    def merge(head, sums):
        top_own = maxes[0, head, 0:1]
        tops = [top_own] + [
            jnp.where(valid[pick], maxes[1 + pick, head, 0:1], NEG) for pick in range(2)
        ]
        top = jnp.maximum(jnp.maximum(tops[0], tops[1]), tops[2])
        ratios = [jnp.exp2((value - top) * SCALE2) for value in tops]
        total = sum(
            ratio * parts[section, head, hd : hd + 1] for section, ratio in enumerate(ratios)
        )
        inverse = 1.0 / total
        shares = [ratio * inverse for ratio in ratios]
        for section in range(3):
            weights[section, head] = jnp.broadcast_to(shares[section], (8, block))
        wide = sum(share * parts[section, head, 0:hd] for section, share in enumerate(shares))
        att_wide[head] = wide
        rounded = wide.astype(BF16).astype(F32)
        upstream = gt[head].astype(F32)
        return (
            sums[0] + jnp.sum(rounded * rounded, axis=0, keepdims=True),
            sums[1] + jnp.sum(rounded * upstream, axis=0, keepdims=True),
        )

    zero_row = jnp.zeros((1, block), F32)
    square_sum, cross_sum = lax.fori_loop(0, group, merge, (zero_row, zero_row))
    stat_send[...] = jnp.concatenate(
        [square_sum, cross_sum, jnp.zeros((6, block), F32)], axis=0
    )
    slot = 2 * y + core
    send(stat_send, stat_recv.at[slot], stat_sems.at[0], stat_sems.at[1], partner)

    @pl.loop(0, far)
    def _(step):
        send(stat_send, stat_recv.at[slot], stat_sems.at[0], stat_sems.at[1], far_member(step))

    stat_recv[slot] = stat_send[...]
    drain(stat_recv.at[pl.ds(0, far + 1)], stat_sems.at[1])
    stats = stat_recv[0]
    for at in range(1, far + 2):
        stats = stats + stat_recv[at]
    features = HEADS * HEAD_DIM
    rscale = lax.rsqrt(stats[0:1] / features + EPSILON)
    factor = rscale * rscale * rscale * (stats[1:2] / features)

    @pl.loop(0, group)
    def _(head):
        wide = att_wide[head]
        rounded = wide.astype(BF16).astype(F32)
        upstream = gt[head].astype(F32)
        grad = (rscale * upstream - rounded * factor).astype(BF16)
        gat[head] = grad
        ga[head] = grad.T
        delta[head] = jnp.broadcast_to(
            jnp.sum(wide * grad.astype(F32), axis=0, keepdims=True), (8, block)
        )

    def value_grad(section):
        dv[...] = jnp.zeros_like(dv)

        @pl.loop(0, group)
        def _(head):
            share = (probs[section, head].astype(F32) * weights[section, head, 0:1]).astype(BF16)
            probs[section, head] = share
            dv[...] += dot(share, ga[head])

    def key_grad(section, first):
        dk[...] = jnp.zeros_like(dk)

        @pl.loop(0, group)
        def _(head):
            dprob = dot(vs[section], gat[head])
            share = probs[section, head].astype(F32)
            dscore = (share * (dprob - delta[head, 0:1])).astype(BF16)
            term = dot(kt[section], dscore)
            if first:
                dqt[head] = term
            else:
                dqt[head] += term
            dk[...] += dot(dscore, qs[:, aligned(head * hd, hd, hd)])

    def give_back(number, pick, source, arrived):
        @pl.loop(1, blocks)
        def _(step):
            to = peer(step)
            send(
                source.at[pick, aligned(piece * to, piece, piece), :],
                arrived.at[pick, my_piece, :],
                hop_send.at[number], hop_recv.at[number], (2 * to + core, y),
            )

        arrived[pick, my_piece, :] = source[pick, my_piece, :]

    for pick in range(2):
        value_grad(1 + pick)
        dv_send[pick] = dv[...].astype(BF16)
        give_back(4 + pick, pick, dv_send, arrived_v)
    for pick in range(2):
        key_grad(1 + pick, pick == 0)
        dk_send[pick] = (dk[...] * SCALE).astype(BF16)
        give_back(6 + pick, pick, dk_send, arrived_k)

    def hand_out(number, buffer, out, lanes):
        send(
            buffer.at[other_rows, :], out.at[:, lanes],
            out_send.at[number], out_recv.at[number], partner,
        )
        keep = pltpu.make_async_copy(
            buffer.at[own_rows, :], out.at[:, lanes], out_local.at[number]
        )
        keep.start()
        return keep

    def settle(number, first_arrival, arrived, totals, home):
        for pick in range(2):
            drain(arrived.at[pick, pl.ds(0, block - piece), :], hop_recv.at[first_arrival + pick])
        totals[...] = (dot(table[0], arrived[0]) + dot(table[1], arrived[1])).astype(BF16)
        target = home.at[aligned(piece * lax.rem(mine, half_blocks), piece, piece), own_head]

        @pl.loop(1, blocks)
        def _(step):
            to = peer(step)
            send(
                totals.at[aligned(piece * to, piece, piece), :], target,
                hop_send.at[number], hop_recv.at[number], (2 * to + upper, y),
            )

        @pl.when(upper != core)
        def _():
            send(
                totals.at[my_piece, :], target,
                hop_send.at[number], hop_recv.at[number], partner,
            )

        @pl.when(upper == core)
        def _():
            pltpu.make_async_copy(totals.at[my_piece, :], target, hop_recv.at[number]).start()

    value_grad(0)
    keeps = [hand_out(0, dv, part_v, own_head)]
    key_grad(0, False)
    dk[...] = dk[...] * SCALE
    keeps.append(hand_out(1, dk, part_k, own_head))
    settle(8, 4, arrived_v, totals_v, home_v)

    @pl.loop(0, group)
    def _(head):
        lanes = aligned(head * hd, hd, hd)
        gq[:, lanes] = (dqt[head] * SCALE).astype(BF16).T

    keeps.append(hand_out(2, gq, gq_out, own_group))

    @pl.loop(0, group)
    def _(head):
        lanes = aligned(head * hd, hd, hd)
        nrm[:, lanes] = (att_wide[head].astype(BF16).astype(F32) * rscale).astype(BF16).T

    keeps.append(hand_out(3, nrm, normed_out, own_group))
    settle(9, 6, arrived_k, totals_k, home_k)

    for number, (src, _) in enumerate(swaps):
        drain(src, swap_send.at[number])
    drain(held_k.at[pl.ds(0, blocks - 1)], hop_send.at[0])
    drain(held_v.at[pl.ds(0, blocks - 1)], hop_send.at[1])
    drain(picked_k.at[pl.ds(0, blocks - 1)], hop_send.at[2])
    drain(picked_v.at[pl.ds(0, blocks - 1)], hop_send.at[3])
    for number in range(4):
        drain(dv_send.at[0, pl.ds(0, block - piece), :], hop_send.at[4 + number])
    drain(stat_recv.at[pl.ds(0, far + 1)], stat_sems.at[0])
    for keep in keeps:
        keep.wait()
    for number, (buffer, out, lanes) in enumerate((
        (dv, part_v, other_head), (dk, part_k, other_head),
        (gq, gq_out, other_group), (nrm, normed_out, other_group),
    )):
        drain(buffer.at[other_rows, :], out_send.at[number])
        drain(out.at[:, lanes], out_recv.at[number])
    for number in (8, 9):
        drain(totals_k.at[pl.ds(0, block - piece), :], hop_send.at[number])

        @pl.when(upper != core)
        def _():
            drain(totals_k.at[my_piece, :], hop_send.at[number])

    drain(home_v, hop_recv.at[8])
    drain(home_k, hop_recv.at[9])


def finish(
    normed_in, gq_in, part_k, part_v, home_k, home_v,
    normed_out, gq_out, gk_out, gv_out,
    wides, parts, homes, grads, in_sems, part_sems, home_sems, out_sems, grad_sems,
):
    chunks = wides.shape[1]
    rows = wides.shape[2]
    loads = []
    stores = []
    for number, (src, dst) in enumerate(((normed_in, normed_out), (gq_in, gq_out))):
        for at in range(chunks):
            span = pl.ds(at * rows, rows)
            held = wides.at[number, at]
            loads.append(pltpu.make_async_copy(src.at[span, :], held, in_sems.at[number, at]))
            stores.append(pltpu.make_async_copy(held, dst.at[span, :], out_sems.at[number, at]))
    terms = []
    for number, (part, home) in enumerate(((part_k, home_k), (part_v, home_v))):
        terms.append((
            pltpu.make_async_copy(part, parts.at[number], part_sems.at[number]),
            pltpu.make_async_copy(home, homes.at[number], home_sems.at[number]),
        ))
    for load in loads:
        load.start()
    for part_load, home_load in terms:
        part_load.start()
        home_load.start()
    for load, store in zip(loads, stores):
        load.wait()
        store.start()
    for number, out in enumerate((gk_out, gv_out)):
        terms[number][0].wait()
        terms[number][1].wait()
        grads[number] = (parts[number] + homes[number].astype(F32)).astype(BF16)
        store = pltpu.make_async_copy(grads.at[number], out, grad_sems.at[number])
        store.start()
        stores.append(store)
    for store in stores:
        store.wait()


def shards(query_rows, key_rows, value_rows, grad_out, chosen):
    blocks = chosen.shape[0]
    rows, kv_width = key_rows.shape
    group = query_rows.shape[1] // kv_width
    kvh = lax.axis_size("kvh")
    hd = HEAD_DIM
    block = 2 * rows
    piece = block // blocks
    width = group * hd
    anywhere = pl.BlockSpec(memory_space=pl.ANY)
    scratch = [
        pltpu.VMEM((block, width), BF16),
        pltpu.VMEM((block, width), BF16),
        pltpu.VMEM((3, block, hd), BF16),
        pltpu.VMEM((3, block, hd), BF16),
        pltpu.VMEM((3, hd + 16, block), BF16),
        pltpu.VMEM((3, hd, block), BF16),
        pltpu.VMEM((group, hd, block), BF16),
        pltpu.VMEM((group, hd, block), BF16),
        pltpu.VMEM((blocks, piece, hd), BF16),
        pltpu.VMEM((blocks, piece, hd), BF16),
        pltpu.VMEM((blocks, 2, piece, hd), BF16),
        pltpu.VMEM((blocks, 2, piece, hd), BF16),
        pltpu.VMEM((3, group, block, block), BF16),
        pltpu.VMEM((3, group, 8, block), F32),
        pltpu.VMEM((3, group, hd + 16, block), F32),
        pltpu.VMEM((3, group, 8, block), F32),
        pltpu.VMEM((group, hd, block), F32),
        pltpu.VMEM((8, block), F32),
        pltpu.VMEM((2 * kvh, 8, block), F32),
        pltpu.VMEM((group, hd, block), BF16),
        pltpu.VMEM((group, block, hd), BF16),
        pltpu.VMEM((group, 8, block), F32),
        pltpu.VMEM((group, hd, block), F32),
        pltpu.VMEM((block, hd), F32),
        pltpu.VMEM((block, hd), F32),
        pltpu.VMEM((2, block, hd), BF16),
        pltpu.VMEM((2, block, hd), BF16),
        pltpu.VMEM((2, block, hd), BF16),
        pltpu.VMEM((2, block, hd), BF16),
        pltpu.VMEM((2, block, block), BF16),
        pltpu.VMEM((block, hd), BF16),
        pltpu.VMEM((block, hd), BF16),
        pltpu.VMEM((block, width), BF16),
        pltpu.VMEM((block, width), BF16),
        pltpu.SemaphoreType.DMA((4,)),
        pltpu.SemaphoreType.DMA((4,)),
        pltpu.SemaphoreType.DMA((4,)),
        pltpu.SemaphoreType.DMA((10,)),
        pltpu.SemaphoreType.DMA((10,)),
        pltpu.SemaphoreType.DMA((2,)),
        pltpu.SemaphoreType.DMA((4,)),
        pltpu.SemaphoreType.DMA((4,)),
        pltpu.SemaphoreType.DMA((4,)),
    ]
    wide = jax.ShapeDtypeStruct(query_rows.shape, BF16)
    part = jax.ShapeDtypeStruct(key_rows.shape, F32)
    thin = jax.ShapeDtypeStruct(key_rows.shape, BF16)
    results = pl.pallas_call(
        functools.partial(kernel, blocks, rows, group, kvh),
        out_shape=(wide, wide, part, part, thin, thin),
        in_specs=[pl.BlockSpec(memory_space=pltpu.SMEM)] + [anywhere] * 4,
        out_specs=(anywhere,) * 6,
        scratch_shapes=scratch,
        compiler_params=pltpu.CompilerParams(
            collective_id=0, has_side_effects=True, vmem_limit_bytes=60 * 2**20
        ),
        name="moba",
    )(chosen.T, query_rows, key_rows, value_rows, grad_out)
    return pl.pallas_call(
        finish,
        out_shape=(wide, wide, thin, thin),
        in_specs=[anywhere] * 6,
        out_specs=(anywhere,) * 4,
        scratch_shapes=[
            pltpu.VMEM((2, 4, rows // 4, query_rows.shape[1]), BF16),
            pltpu.VMEM((2, *key_rows.shape), F32),
            pltpu.VMEM((2, *key_rows.shape), BF16),
            pltpu.VMEM((2, *key_rows.shape), BF16),
            pltpu.SemaphoreType.DMA((2, 4)),
            pltpu.SemaphoreType.DMA((2,)),
            pltpu.SemaphoreType.DMA((2,)),
            pltpu.SemaphoreType.DMA((2, 4)),
            pltpu.SemaphoreType.DMA((2,)),
        ],
        name="finish",
    )(*results)


def solution(mesh):
    return jax.shard_map(
        shards,
        mesh=mesh,
        in_specs=(P("ctx", "kvh"), P("ctx", "kvh"), P("ctx", "kvh"), P("ctx", "kvh"), P()),
        out_specs=(P("ctx", "kvh"), P("ctx", "kvh"), P("ctx", "kvh"), P("ctx", "kvh")),
        check_vma=False,
    )
```

time: 81.1 us -> 70.2 us (0.87)
  local copies, waits for them, and re-layouts: 5.92 us -> 0 us
  Pallas kernels: 74.3 us -> 69.4 us
    pallas_call x1, Pallas kernels: 74.3 us -> 67 us  [shards(): pl.pallas_call(functools.partial(kernel, blocks, rows, group, kvh), out_s...]
    unnamed x11 -> x0, local copies, waits for them, and re-layouts: 5.92 us -> none
    pallas_call x0 -> x1, Pallas kernels: none -> 2.39 us  [shards(): pl.pallas_call(finish, out_shape=(wide, wide, thin, thin), in_specs=[anyw...]
where the time goes in v1:
time: 70.2 us; the launch traced here: 70.1 us
  Pallas kernels  69.4 us (99%)
    pallas_call x1, Pallas kernels, shards(): pl.pallas_call(functools.partial(kernel, blocks, rows, group, kvh), out_s...  67 us
    pallas_call x1, Pallas kernels, shards(): pl.pallas_call(finish, out_shape=(wide, wide, thin, thin), in_specs=[anyw...  2.39 us

profile of v1, /device:TPU:1, one launch (start us, length us, event | category | flops | bytes accessed | tf_op | source)
XLA Modules:
  0.0 70.1 jit_solution(9371856746207029750)
XLA Ops:
  0.6 67.0 %moba.1 = (bf16[256,1024]{1,0:T(8,128)(2,1)}, bf16[256,1024]{1,0:T(8,128)(2,1)}, f32[256,256]{1,0:T(8,128)}, f32[256,256]{1,0:T(8,128)}, bf16[256,256]{1,0:T(8,128)(2,1)}, /*index=5*/bf16[256,256]{1,0:T(8,128)(2,1)}) custom-call(s32[2,32]{1,0:T(2,128)} %bitcast.1, bf16[256,1024]{1,0:T(8,128)(2,1)} %q_in.1, bf16[256,256]{1,0:T(8,128)(2,1)} %k_in.1, ...), custom_call_target="tpu_custom_call" | custom-call | tf_op jit(solution)/shard_map/moba/pallas_call | solution.py:508
  67.7 2.4 %finish.1 = (bf16[256,1024]{1,0:T(8,128)(2,1)}, bf16[256,1024]{1,0:T(8,128)(2,1)}, bf16[256,256]{1,0:T(8,128)(2,1)}, bf16[256,256]{1,0:T(8,128)(2,1)}) custom-call(bf16[256,1024]{1,0:T(8,128)(2,1)} %get-tuple-element.10.normed_in, bf16[256,1024]{1,0:T(8,128)(2,1)} %get-tuple-element.11.gq_in, f32[256,256]{1,0:T(8,128)} %get-tuple-element.12.part_k, ...), custom_call_target="tpu_custom_call" | custom-call | tf_op jit(solution)/shard_map/finish/pallas_call | solution.py:519

commit v2 on v1

--- a/solution.py
+++ b/solution.py
@@ -31,8 +31,8 @@
     blocks, rows, group, kvh,
     chosen, q_in, k_in, v_in, g_in,
     normed_out, gq_out, part_k, part_v, home_k, home_v,
-    qs, gos, ks, vs, vtx, kt, qt, gt, held_k, held_v, picked_k, picked_v, probs, maxes, parts,
-    weights, att_wide, stat_send, stat_recv, gat, ga, delta, dqt, dk, dv, dk_send, dv_send,
+    qs, gos, ks, vs, vtx, kt, qh, qt, gt, held_k, held_v, picked_k, picked_v, probs, maxes, parts,
+    weights, att_wide, stat_send, stat_recv, gat, ga, delta, dscores, dk, dv, dk_send, dv_send,
     arrived_k, arrived_v, table, totals_k, totals_v, nrm, gq,
     local_sem, swap_send, swap_recv, hop_send, hop_recv, stat_sems, out_local, out_send, out_recv,
 ):
@@ -103,8 +103,13 @@
         (q_in.at[:, other_group], qs.at[own_rows, :]),
         (g_in.at[:, other_group], gos.at[own_rows, :]),
     ]
-    for number, (src, dst) in enumerate(swaps):
+
+    def swap(number):
+        src, dst = swaps[number]
         send(src, dst, swap_send.at[number], swap_recv.at[number], partner)
+
+    swap(0)
+    swap(1)
 
     def scatter(number, source, held):
         def scatter_half(half):
@@ -126,18 +131,24 @@
         held[mine] = source[0, my_piece, :]
 
     scatter(0, ks, held_k)
+    drain(held_k.at[pl.ds(0, blocks - 1)], hop_send.at[0])
     scatter(1, vs, held_v)
+    swap(2)
+    swap(3)
 
     for number, target in ((2, qs), (3, gos)):
         fetches[number].wait()
         drain(target.at[other_rows, :], swap_recv.at[number])
 
     def turn_keys(section):
-        kt[section] = ks[section].T
+        kt[:, section * block : (section + 1) * block] = ks[section].T
 
     def turn_values(section):
         vtx[section, 0:hd, :] = vs[section].T
         vtx[section, hd : hd + 16, :] = jnp.ones((16, block), BF16)
+
+    def head_lanes(head):
+        return aligned(head * block, block, block)
 
     def score(section, head):
         scores = dot(ks[section], qt[head])
@@ -149,44 +160,61 @@
             scores = jnp.where(key_order <= row_order, scores, NEG)
         top = jnp.max(scores, axis=0, keepdims=True)
         terms = jnp.exp2((scores - top) * SCALE2).astype(BF16)
-        probs[section, head] = terms
+        probs[section, :, head_lanes(head)] = terms
         maxes[section, head] = jnp.broadcast_to(top, (8, block))
         return terms
 
-    def deliver(number, held, picked, target):
-        drain(held.at[pl.ds(0, blocks - 1)], hop_recv.at[number])
+    def deliver_keys():
+        drain(held_k.at[pl.ds(0, blocks - 1)], hop_recv.at[0])
 
         @pl.loop(1, blocks)
         def _(step):
             to = peer(step)
             for pick in range(2):
-                picked[to, pick] = held[chosen[pick, to]]
+                picked_k[to, pick] = held_k[chosen[pick, to]]
             send(
-                picked.at[to], target.at[pl.ds(1, 2), my_piece, :],
-                hop_send.at[2 + number], hop_recv.at[2 + number], (2 * to + core, y),
+                picked_k.at[to], ks.at[pl.ds(1, 2), my_piece, :],
+                hop_send.at[2], hop_recv.at[2], (2 * to + core, y),
             )
 
         for pick in range(2):
-            target[1 + pick, my_piece, :] = held[chosen[pick, mine]]
+            ks[1 + pick, my_piece, :] = held_k[chosen[pick, mine]]
+
+    def deliver_values(pick):
+        @pl.loop(1, blocks)
+        def _(step):
+            to = peer(step)
+            picked_v[pick, to] = held_v[chosen[pick, to]]
+            send(
+                picked_v.at[pick, to], vs.at[1 + pick, my_piece, :],
+                hop_send.at[3 + pick], hop_recv.at[3 + pick], (2 * to + core, y),
+            )
+
+        vs[1 + pick, my_piece, :] = held_v[chosen[pick, mine]]
 
     turn_keys(0)
 
     @pl.loop(0, group)
     def _(head):
-        qt[head] = qs[:, aligned(head * hd, hd, hd)].T
-
-    deliver(0, held_k, picked_k, ks)
+        queries = qs[:, aligned(head * hd, hd, hd)]
+        qh[aligned(head * block, block, block), :] = queries
+        qt[head] = queries.T
+
+    drain(held_v.at[pl.ds(0, blocks - 1)], hop_send.at[1])
+    deliver_keys()
     turn_values(0)
 
     @pl.loop(0, group)
     def _(head):
         gt[head] = gos[:, aligned(head * hd, hd, hd)].T
 
-    deliver(1, held_v, picked_v, vs)
-
     @pl.loop(0, group)
     def _(head):
         parts[0, head] = dot(vtx[0], score(0, head))
+
+    drain(held_v.at[pl.ds(0, blocks - 1)], hop_recv.at[1])
+    drain(picked_k.at[pl.ds(0, blocks - 1)], hop_send.at[2])
+    deliver_values(0)
 
     for pick in range(2):
         lane_owner = lax.broadcasted_iota(jnp.int32, (8, block), 1) // piece
@@ -202,6 +230,8 @@
         wanted = owners[0:1] * piece + lax.rem(lane_at, piece)
         table[pick] = (row_at == wanted).astype(F32).astype(BF16)
 
+    drain(picked_v.at[0, pl.ds(0, blocks - 1)], hop_send.at[3])
+    deliver_values(1)
     drain(ks.at[pl.ds(1, 2), pl.ds(0, block - piece), :], hop_recv.at[2])
     for pick in range(2):
         @pl.loop(0, group)
@@ -210,13 +240,13 @@
 
         turn_keys(1 + pick)
 
-    drain(vs.at[pl.ds(1, 2), pl.ds(0, block - piece), :], hop_recv.at[3])
     for pick in range(2):
+        drain(vs.at[1 + pick, pl.ds(0, block - piece), :], hop_recv.at[3 + pick])
         turn_values(1 + pick)
 
         @pl.loop(0, group)
         def _(head):
-            parts[1 + pick, head] = dot(vtx[1 + pick], probs[1 + pick, head])
+            parts[1 + pick, head] = dot(vtx[1 + pick], probs[1 + pick, :, head_lanes(head)])
 
     valid = [chosen[pick, mine] < mine for pick in range(2)]
 
@@ -245,8 +275,14 @@
 
     zero_row = jnp.zeros((1, block), F32)
     square_sum, cross_sum = lax.fori_loop(0, group, merge, (zero_row, zero_row))
+    folds = block // 128
     stat_send[...] = jnp.concatenate(
-        [square_sum, cross_sum, jnp.zeros((6, block), F32)], axis=0
+        [
+            total[:, at * 128 : (at + 1) * 128]
+            for total in (square_sum, cross_sum)
+            for at in range(folds)
+        ],
+        axis=0,
     )
     slot = 2 * y + core
     send(stat_send, stat_recv.at[slot], stat_sems.at[0], stat_sems.at[1], partner)
@@ -256,13 +292,23 @@
         send(stat_send, stat_recv.at[slot], stat_sems.at[0], stat_sems.at[1], far_member(step))
 
     stat_recv[slot] = stat_send[...]
+
+    @pl.loop(0, group)
+    def _(head):
+        lanes = head_lanes(head)
+        for section in range(3):
+            share = probs[section, :, lanes].astype(F32) * weights[section, head, 0:1]
+            probs[section, :, lanes] = share.astype(BF16)
+
     drain(stat_recv.at[pl.ds(0, far + 1)], stat_sems.at[1])
     stats = stat_recv[0]
     for at in range(1, far + 2):
         stats = stats + stat_recv[at]
     features = HEADS * HEAD_DIM
-    rscale = lax.rsqrt(stats[0:1] / features + EPSILON)
-    factor = rscale * rscale * rscale * (stats[1:2] / features)
+    square_row = jnp.concatenate([stats[at : at + 1] for at in range(folds)], axis=1)
+    cross_row = jnp.concatenate([stats[folds + at : folds + at + 1] for at in range(folds)], axis=1)
+    rscale = lax.rsqrt(square_row / features + EPSILON)
+    factor = rscale * rscale * rscale * (cross_row / features)
 
     @pl.loop(0, group)
     def _(head):
@@ -271,34 +317,24 @@
         upstream = gt[head].astype(F32)
         grad = (rscale * upstream - rounded * factor).astype(BF16)
         gat[head] = grad
-        ga[head] = grad.T
+        ga[head_lanes(head), :] = grad.T
         delta[head] = jnp.broadcast_to(
             jnp.sum(wide * grad.astype(F32), axis=0, keepdims=True), (8, block)
         )
 
     def value_grad(section):
-        dv[...] = jnp.zeros_like(dv)
-
+        return dot(probs[section], ga[...])
+
+    def key_grad(section):
         @pl.loop(0, group)
         def _(head):
-            share = (probs[section, head].astype(F32) * weights[section, head, 0:1]).astype(BF16)
-            probs[section, head] = share
-            dv[...] += dot(share, ga[head])
-
-    def key_grad(section, first):
-        dk[...] = jnp.zeros_like(dk)
-
-        @pl.loop(0, group)
-        def _(head):
+            lanes = head_lanes(head)
             dprob = dot(vs[section], gat[head])
-            share = probs[section, head].astype(F32)
+            share = probs[section, :, lanes].astype(F32)
             dscore = (share * (dprob - delta[head, 0:1])).astype(BF16)
-            term = dot(kt[section], dscore)
-            if first:
-                dqt[head] = term
-            else:
-                dqt[head] += term
-            dk[...] += dot(dscore, qs[:, aligned(head * hd, hd, hd)])
+            dscores[section * block : (section + 1) * block, lanes] = dscore
+
+        return dot(dscores[section * block : (section + 1) * block, :], qh[...]) * SCALE
 
     def give_back(number, pick, source, arrived):
         @pl.loop(1, blocks)
@@ -313,13 +349,11 @@
         arrived[pick, my_piece, :] = source[pick, my_piece, :]
 
     for pick in range(2):
-        value_grad(1 + pick)
-        dv_send[pick] = dv[...].astype(BF16)
-        give_back(4 + pick, pick, dv_send, arrived_v)
+        dv_send[pick] = value_grad(1 + pick).astype(BF16)
+        give_back(5 + pick, pick, dv_send, arrived_v)
     for pick in range(2):
-        key_grad(1 + pick, pick == 0)
-        dk_send[pick] = (dk[...] * SCALE).astype(BF16)
-        give_back(6 + pick, pick, dk_send, arrived_k)
+        dk_send[pick] = key_grad(1 + pick).astype(BF16)
+        give_back(7 + pick, pick, dk_send, arrived_k)
 
     def hand_out(number, buffer, out, lanes):
         send(
@@ -332,9 +366,9 @@
         keep.start()
         return keep
 
-    def settle(number, first_arrival, arrived, totals, home):
+    def settle(number, arrival, arrived, totals, home):
         for pick in range(2):
-            drain(arrived.at[pick, pl.ds(0, block - piece), :], hop_recv.at[first_arrival + pick])
+            drain(arrived.at[pick, pl.ds(0, block - piece), :], hop_recv.at[arrival + pick])
         totals[...] = (dot(table[0], arrived[0]) + dot(table[1], arrived[1])).astype(BF16)
         target = home.at[aligned(piece * lax.rem(mine, half_blocks), piece, piece), own_head]
 
@@ -357,17 +391,17 @@
         def _():
             pltpu.make_async_copy(totals.at[my_piece, :], target, hop_recv.at[number]).start()
 
-    value_grad(0)
+    dv[...] = value_grad(0)
     keeps = [hand_out(0, dv, part_v, own_head)]
-    key_grad(0, False)
-    dk[...] = dk[...] * SCALE
+    dk[...] = key_grad(0)
     keeps.append(hand_out(1, dk, part_k, own_head))
-    settle(8, 4, arrived_v, totals_v, home_v)
+    settle(9, 5, arrived_v, totals_v, home_v)
 
     @pl.loop(0, group)
     def _(head):
         lanes = aligned(head * hd, hd, hd)
-        gq[:, lanes] = (dqt[head] * SCALE).astype(BF16).T
+        grad = dot(kt[...], dscores[:, head_lanes(head)]) * SCALE
+        gq[:, lanes] = grad.astype(BF16).T
 
     keeps.append(hand_out(2, gq, gq_out, own_group))
 
@@ -377,16 +411,14 @@
         nrm[:, lanes] = (att_wide[head].astype(BF16).astype(F32) * rscale).astype(BF16).T
 
     keeps.append(hand_out(3, nrm, normed_out, own_group))
-    settle(9, 6, arrived_k, totals_k, home_k)
+    settle(10, 7, arrived_k, totals_k, home_k)
 
     for number, (src, _) in enumerate(swaps):
         drain(src, swap_send.at[number])
-    drain(held_k.at[pl.ds(0, blocks - 1)], hop_send.at[0])
-    drain(held_v.at[pl.ds(0, blocks - 1)], hop_send.at[1])
-    drain(picked_k.at[pl.ds(0, blocks - 1)], hop_send.at[2])
-    drain(picked_v.at[pl.ds(0, blocks - 1)], hop_send.at[3])
-    for number in range(4):
-        drain(dv_send.at[0, pl.ds(0, block - piece), :], hop_send.at[4 + number])
+    drain(picked_v.at[1, pl.ds(0, blocks - 1)], hop_send.at[4])
+    for number, buffer in ((5, dv_send), (7, dk_send)):
+        for pick in range(2):
+            drain(buffer.at[pick, pl.ds(0, block - piece), :], hop_send.at[number + pick])
     drain(stat_recv.at[pl.ds(0, far + 1)], stat_sems.at[0])
     for keep in keeps:
         keep.wait()
@@ -396,15 +428,15 @@
     )):
         drain(buffer.at[other_rows, :], out_send.at[number])
         drain(out.at[:, lanes], out_recv.at[number])
-    for number in (8, 9):
+    for number in (9, 10):
         drain(totals_k.at[pl.ds(0, block - piece), :], hop_send.at[number])
 
         @pl.when(upper != core)
         def _():
             drain(totals_k.at[my_piece, :], hop_send.at[number])
 
-    drain(home_v, hop_recv.at[8])
-    drain(home_k, hop_recv.at[9])
+    drain(home_v, hop_recv.at[9])
+    drain(home_k, hop_recv.at[10])
 
 
 def finish(
@@ -463,24 +495,25 @@
         pltpu.VMEM((3, block, hd), BF16),
         pltpu.VMEM((3, block, hd), BF16),
         pltpu.VMEM((3, hd + 16, block), BF16),
-        pltpu.VMEM((3, hd, block), BF16),
+        pltpu.VMEM((hd, 3 * block), BF16),
+        pltpu.VMEM((group * block, hd), BF16),
         pltpu.VMEM((group, hd, block), BF16),
         pltpu.VMEM((group, hd, block), BF16),
         pltpu.VMEM((blocks, piece, hd), BF16),
         pltpu.VMEM((blocks, piece, hd), BF16),
         pltpu.VMEM((blocks, 2, piece, hd), BF16),
-        pltpu.VMEM((blocks, 2, piece, hd), BF16),
-        pltpu.VMEM((3, group, block, block), BF16),
+        pltpu.VMEM((2, blocks, piece, hd), BF16),
+        pltpu.VMEM((3, block, group * block), BF16),
         pltpu.VMEM((3, group, 8, block), F32),
         pltpu.VMEM((3, group, hd + 16, block), F32),
         pltpu.VMEM((3, group, 8, block), F32),
         pltpu.VMEM((group, hd, block), F32),
-        pltpu.VMEM((8, block), F32),
-        pltpu.VMEM((2 * kvh, 8, block), F32),
+        pltpu.VMEM((2 * block // 128, 128), F32),
+        pltpu.VMEM((2 * kvh, 2 * block // 128, 128), F32),
         pltpu.VMEM((group, hd, block), BF16),
-        pltpu.VMEM((group, block, hd), BF16),
+        pltpu.VMEM((group * block, hd), BF16),
         pltpu.VMEM((group, 8, block), F32),
-        pltpu.VMEM((group, hd, block), F32),
+        pltpu.VMEM((3 * block, group * block), BF16),
         pltpu.VMEM((block, hd), F32),
         pltpu.VMEM((block, hd), F32),
         pltpu.VMEM((2, block, hd), BF16),
@@ -495,8 +528,8 @@
         pltpu.SemaphoreType.DMA((4,)),
         pltpu.SemaphoreType.DMA((4,)),
         pltpu.SemaphoreType.DMA((4,)),
-        pltpu.SemaphoreType.DMA((10,)),
-        pltpu.SemaphoreType.DMA((10,)),
+        pltpu.SemaphoreType.DMA((11,)),
+        pltpu.SemaphoreType.DMA((11,)),
         pltpu.SemaphoreType.DMA((2,)),
         pltpu.SemaphoreType.DMA((4,)),
         pltpu.SemaphoreType.DMA((4,)),
@@ -522,7 +555,7 @@
         in_specs=[anywhere] * 6,
         out_specs=(anywhere,) * 4,
         scratch_shapes=[
-            pltpu.VMEM((2, 4, rows // 4, query_rows.shape[1]), BF16),
+            pltpu.VMEM((2, 1, rows, query_rows.shape[1]), BF16),
             pltpu.VMEM((2, *key_rows.shape), F32),
             pltpu.VMEM((2, *key_rows.shape), BF16),
             pltpu.VMEM((2, *key_rows.shape), BF16),

time: 70.2 us -> 69.2 us (0.986)
  Pallas kernels: 69.4 us -> 68.4 us
    pallas_call x1, Pallas kernels: 67 us -> 66.1 us  [shards(): pl.pallas_call(functools.partial(kernel, blocks, rows, group, kvh), out_s...]
where the time goes in v2:
time: 69.2 us; the launch traced here: 69.1 us
  Pallas kernels  68.4 us (99%)
    pallas_call x1, Pallas kernels, shards(): pl.pallas_call(functools.partial(kernel, blocks, rows, group, kvh), out_s...  66.1 us
    pallas_call x1, Pallas kernels, shards(): pl.pallas_call(finish, out_shape=(wide, wide, thin, thin), in_specs=[anyw...  2.38 us

profile of v2, /device:TPU:1, one launch (start us, length us, event | category | flops | bytes accessed | tf_op | source)
XLA Modules:
  0.0 69.1 jit_solution(554055902517229994)
XLA Ops:
  0.6 66.1 %moba.1 = (bf16[256,1024]{1,0:T(8,128)(2,1)}, bf16[256,1024]{1,0:T(8,128)(2,1)}, f32[256,256]{1,0:T(8,128)}, f32[256,256]{1,0:T(8,128)}, bf16[256,256]{1,0:T(8,128)(2,1)}, /*index=5*/bf16[256,256]{1,0:T(8,128)(2,1)}) custom-call(s32[2,32]{1,0:T(2,128)} %bitcast.1, bf16[256,1024]{1,0:T(8,128)(2,1)} %q_in.1, bf16[256,256]{1,0:T(8,128)(2,1)} %k_in.1, ...), custom_call_target="tpu_custom_call" | custom-call | tf_op jit(solution)/shard_map/moba/pallas_call | solution.py:541
  66.7 2.4 %finish.1 = (bf16[256,1024]{1,0:T(8,128)(2,1)}, bf16[256,1024]{1,0:T(8,128)(2,1)}, bf16[256,256]{1,0:T(8,128)(2,1)}, bf16[256,256]{1,0:T(8,128)(2,1)}) custom-call(bf16[256,1024]{1,0:T(8,128)(2,1)} %get-tuple-element.10.normed_in, bf16[256,1024]{1,0:T(8,128)(2,1)} %get-tuple-element.11.gq_in, f32[256,256]{1,0:T(8,128)} %get-tuple-element.12.part_k, ...), custom_call_target="tpu_custom_call" | custom-call | tf_op jit(solution)/shard_map/finish/pallas_call | solution.py:552

commit v3 on v2

--- a/solution.py
+++ b/solution.py
@@ -194,7 +194,7 @@
 
     turn_keys(0)
 
-    @pl.loop(0, group)
+    @pl.loop(0, group, unroll=2)
     def _(head):
         queries = qs[:, aligned(head * hd, hd, hd)]
         qh[aligned(head * block, block, block), :] = queries
@@ -204,16 +204,15 @@
     deliver_keys()
     turn_values(0)
 
-    @pl.loop(0, group)
+    @pl.loop(0, group, unroll=2)
     def _(head):
         gt[head] = gos[:, aligned(head * hd, hd, hd)].T
 
-    @pl.loop(0, group)
+    @pl.loop(0, group, unroll=2)
     def _(head):
         parts[0, head] = dot(vtx[0], score(0, head))
 
     drain(held_v.at[pl.ds(0, blocks - 1)], hop_recv.at[1])
-    drain(picked_k.at[pl.ds(0, blocks - 1)], hop_send.at[2])
     deliver_values(0)
 
     for pick in range(2):
@@ -230,11 +229,10 @@
         wanted = owners[0:1] * piece + lax.rem(lane_at, piece)
         table[pick] = (row_at == wanted).astype(F32).astype(BF16)
 
-    drain(picked_v.at[0, pl.ds(0, blocks - 1)], hop_send.at[3])
     deliver_values(1)
     drain(ks.at[pl.ds(1, 2), pl.ds(0, block - piece), :], hop_recv.at[2])
     for pick in range(2):
-        @pl.loop(0, group)
+        @pl.loop(0, group, unroll=2)
         def _(head):
             score(1 + pick, head)
 
@@ -244,7 +242,7 @@
         drain(vs.at[1 + pick, pl.ds(0, block - piece), :], hop_recv.at[3 + pick])
         turn_values(1 + pick)
 
-        @pl.loop(0, group)
+        @pl.loop(0, group, unroll=2)
         def _(head):
             parts[1 + pick, head] = dot(vtx[1 + pick], probs[1 + pick, :, head_lanes(head)])
 
@@ -293,7 +291,7 @@
 
     stat_recv[slot] = stat_send[...]
 
-    @pl.loop(0, group)
+    @pl.loop(0, group, unroll=2)
     def _(head):
         lanes = head_lanes(head)
         for section in range(3):
@@ -310,7 +308,7 @@
     rscale = lax.rsqrt(square_row / features + EPSILON)
     factor = rscale * rscale * rscale * (cross_row / features)
 
-    @pl.loop(0, group)
+    @pl.loop(0, group, unroll=2)
     def _(head):
         wide = att_wide[head]
         rounded = wide.astype(BF16).astype(F32)
@@ -326,7 +324,7 @@
         return dot(probs[section], ga[...])
 
     def key_grad(section):
-        @pl.loop(0, group)
+        @pl.loop(0, group, unroll=2)
         def _(head):
             lanes = head_lanes(head)
             dprob = dot(vs[section], gat[head])
@@ -397,25 +395,27 @@
     keeps.append(hand_out(1, dk, part_k, own_head))
     settle(9, 5, arrived_v, totals_v, home_v)
 
-    @pl.loop(0, group)
+    @pl.loop(0, group, unroll=2)
     def _(head):
         lanes = aligned(head * hd, hd, hd)
         grad = dot(kt[...], dscores[:, head_lanes(head)]) * SCALE
         gq[:, lanes] = grad.astype(BF16).T
 
-    keeps.append(hand_out(2, gq, gq_out, own_group))
-
-    @pl.loop(0, group)
+
+    @pl.loop(0, group, unroll=2)
     def _(head):
         lanes = aligned(head * hd, hd, hd)
         nrm[:, lanes] = (att_wide[head].astype(BF16).astype(F32) * rscale).astype(BF16).T
 
+    settle(10, 7, arrived_k, totals_k, home_k)
+    keeps.append(hand_out(2, gq, gq_out, own_group))
     keeps.append(hand_out(3, nrm, normed_out, own_group))
-    settle(10, 7, arrived_k, totals_k, home_k)
 
     for number, (src, _) in enumerate(swaps):
         drain(src, swap_send.at[number])
     drain(picked_v.at[1, pl.ds(0, blocks - 1)], hop_send.at[4])
+    drain(picked_k.at[pl.ds(0, blocks - 1)], hop_send.at[2])
+    drain(picked_v.at[0, pl.ds(0, blocks - 1)], hop_send.at[3])
     for number, buffer in ((5, dv_send), (7, dk_send)):
         for pick in range(2):
             drain(buffer.at[pick, pl.ds(0, block - piece), :], hop_send.at[number + pick])

time: 69.2 us -> 68.1 us (0.984)
  Pallas kernels: 68.4 us -> 67.3 us
    pallas_call x1, Pallas kernels: 66.1 us -> 64.9 us  [shards(): pl.pallas_call(functools.partial(kernel, blocks, rows, group, kvh), out_s...]
where the time goes in v3:
time: 68.1 us; the launch traced here: 67.9 us
  Pallas kernels  67.3 us (99%)
    pallas_call x1, Pallas kernels, shards(): pl.pallas_call(functools.partial(kernel, blocks, rows, group, kvh), out_s...  64.9 us
    pallas_call x1, Pallas kernels, shards(): pl.pallas_call(finish, out_shape=(wide, wide, thin, thin), in_specs=[anyw...  2.38 us

profile of v3, /device:TPU:1, one launch (start us, length us, event | category | flops | bytes accessed | tf_op | source)
XLA Modules:
  0.0 67.9 jit_solution(16186367149843018251)
XLA Ops:
  0.6 64.9 %moba.1 = (bf16[256,1024]{1,0:T(8,128)(2,1)}, bf16[256,1024]{1,0:T(8,128)(2,1)}, f32[256,256]{1,0:T(8,128)}, f32[256,256]{1,0:T(8,128)}, bf16[256,256]{1,0:T(8,128)(2,1)}, /*index=5*/bf16[256,256]{1,0:T(8,128)(2,1)}) custom-call(s32[2,32]{1,0:T(2,128)} %bitcast.1, bf16[256,1024]{1,0:T(8,128)(2,1)} %q_in.1, bf16[256,256]{1,0:T(8,128)(2,1)} %k_in.1, ...), custom_call_target="tpu_custom_call" | custom-call | tf_op jit(solution)/shard_map/moba/pallas_call | solution.py:541
  65.5 2.4 %finish.1 = (bf16[256,1024]{1,0:T(8,128)(2,1)}, bf16[256,1024]{1,0:T(8,128)(2,1)}, bf16[256,256]{1,0:T(8,128)(2,1)}, bf16[256,256]{1,0:T(8,128)(2,1)}) custom-call(bf16[256,1024]{1,0:T(8,128)(2,1)} %get-tuple-element.10.normed_in, bf16[256,1024]{1,0:T(8,128)(2,1)} %get-tuple-element.11.gq_in, f32[256,256]{1,0:T(8,128)} %get-tuple-element.12.part_k, ...), custom_call_target="tpu_custom_call" | custom-call | tf_op jit(solution)/shard_map/finish/pallas_call | solution.py:552

commit v4 on v3

--- a/solution.py
+++ b/solution.py
@@ -215,20 +215,6 @@
     drain(held_v.at[pl.ds(0, blocks - 1)], hop_recv.at[1])
     deliver_values(0)
 
-    for pick in range(2):
-        lane_owner = lax.broadcasted_iota(jnp.int32, (8, block), 1) // piece
-
-        def fill(reader, owners):
-            choice = chosen[pick, reader]
-            choice = jnp.where(choice < reader, choice, -1)
-            return jnp.where(lane_owner == reader, choice, owners)
-
-        owners = lax.fori_loop(0, blocks, fill, jnp.full((8, block), -1, jnp.int32))
-        row_at = lax.broadcasted_iota(jnp.int32, (block, block), 0)
-        lane_at = lax.broadcasted_iota(jnp.int32, (block, block), 1)
-        wanted = owners[0:1] * piece + lax.rem(lane_at, piece)
-        table[pick] = (row_at == wanted).astype(F32).astype(BF16)
-
     deliver_values(1)
     drain(ks.at[pl.ds(1, 2), pl.ds(0, block - piece), :], hop_recv.at[2])
     for pick in range(2):
@@ -297,6 +283,20 @@
         for section in range(3):
             share = probs[section, :, lanes].astype(F32) * weights[section, head, 0:1]
             probs[section, :, lanes] = share.astype(BF16)
+
+    for pick in range(2):
+        lane_owner = lax.broadcasted_iota(jnp.int32, (8, block), 1) // piece
+
+        def fill(reader, owners):
+            choice = chosen[pick, reader]
+            choice = jnp.where(choice < reader, choice, -1)
+            return jnp.where(lane_owner == reader, choice, owners)
+
+        owners = lax.fori_loop(0, blocks, fill, jnp.full((8, block), -1, jnp.int32))
+        row_at = lax.broadcasted_iota(jnp.int32, (block, block), 0)
+        lane_at = lax.broadcasted_iota(jnp.int32, (block, block), 1)
+        wanted = owners[0:1] * piece + lax.rem(lane_at, piece)
+        table[pick] = (row_at == wanted).astype(F32).astype(BF16)
 
     drain(stat_recv.at[pl.ds(0, far + 1)], stat_sems.at[1])
     stats = stat_recv[0]

time: 68.1 us -> 68.1 us (level)
  no operation moved by 1% of the time
where the time goes in v4:
time: 68.1 us; the launch traced here: 67.9 us
  Pallas kernels  67.3 us (99%)
    pallas_call x1, Pallas kernels, shards(): pl.pallas_call(functools.partial(kernel, blocks, rows, group, kvh), out_s...  64.9 us
    pallas_call x1, Pallas kernels, shards(): pl.pallas_call(finish, out_shape=(wide, wide, thin, thin), in_specs=[anyw...  2.38 us

profile of v4, /device:TPU:1, one launch (start us, length us, event | category | flops | bytes accessed | tf_op | source)
XLA Modules:
  0.0 67.9 jit_solution(4783814581723845495)
XLA Ops:
  0.6 64.9 %moba.1 = (bf16[256,1024]{1,0:T(8,128)(2,1)}, bf16[256,1024]{1,0:T(8,128)(2,1)}, f32[256,256]{1,0:T(8,128)}, f32[256,256]{1,0:T(8,128)}, bf16[256,256]{1,0:T(8,128)(2,1)}, /*index=5*/bf16[256,256]{1,0:T(8,128)(2,1)}) custom-call(s32[2,32]{1,0:T(2,128)} %bitcast.1, bf16[256,1024]{1,0:T(8,128)(2,1)} %q_in.1, bf16[256,256]{1,0:T(8,128)(2,1)} %k_in.1, ...), custom_call_target="tpu_custom_call" | custom-call | tf_op jit(solution)/shard_map/moba/pallas_call | solution.py:541
  65.6 2.4 %finish.1 = (bf16[256,1024]{1,0:T(8,128)(2,1)}, bf16[256,1024]{1,0:T(8,128)(2,1)}, bf16[256,256]{1,0:T(8,128)(2,1)}, bf16[256,256]{1,0:T(8,128)(2,1)}) custom-call(bf16[256,1024]{1,0:T(8,128)(2,1)} %get-tuple-element.10.normed_in, bf16[256,1024]{1,0:T(8,128)(2,1)} %get-tuple-element.11.gq_in, f32[256,256]{1,0:T(8,128)} %get-tuple-element.12.part_k, ...), custom_call_target="tpu_custom_call" | custom-call | tf_op jit(solution)/shard_map/finish/pallas_call | solution.py:552
